TPU v7x, 512 devices: a whole 4x8x8 slice. The times are simulated.
512 devices in a mesh: group: 8 (over x, z_lo), shard: 64 (over z_hi, y, core).
Axes of the slice: x: 4, y: 8, z: 8 (z_hi: 4, z_lo: 2; z = z_hi * 2 + z_lo), core: 2. Of those that a mesh axis runs over, the one named last changes fastest.
Arguments:
- tokens: bfloat16 [512, 3072], P('group', 'shard'), may hold values from -6 to 6
- cotangent: bfloat16 [512, 3072], P('group', 'shard'), may hold values from -1.5 to 1.5
- expert_ids: int32 [512, 2], P('group'), may hold values from 0 to 7, all different within a row; in each aligned block of 64 rows (0 to 63, 64 to 127, ...) at most 36 rows name the same one
- route_weight: float32 [512, 2], P('group'), may hold values from 0.1 to 0.9
- w_gate: bfloat16 [8, 3072, 8192], P('group', None, 'shard'), may hold values from -0.109375 to 0.109375
- w_up: bfloat16 [8, 3072, 8192], P('group', None, 'shard'), may hold values from -0.109375 to 0.109375
- w_down: bfloat16 [8, 8192, 3072], P('group', 'shard'), may hold values from -0.109375 to 0.109375
Outputs:
- grad_tokens: bfloat16 [512, 3072], P('group', 'shard')
- grad_gate: bfloat16 [8, 3072, 8192], P('group', None, 'shard')
- grad_up: bfloat16 [8, 3072, 8192], P('group', None, 'shard')
Inputs may be any that keep to these rules, and one draw needn't show every extreme that they name: `expert_ids`: each token names 2 different experts. Among the 64 tokens of one aligned block (the tokens of one index of group), no expert is named by more than 36 tokens.
All inputs are finite; a program needn't handle non-finite values.
Results may differ from a plain program's by a relative error of at most 0.0064.
Values may be sent and summed in bfloat16 or wider, within the bound.
A program may use at most 64 MiB of HBM per device.

v0:
```python
import jax
import jax.numpy as jnp
from jax import lax
from jax.sharding import PartitionSpec as P

EXPERTS = 8
CAP = 36
exact_mode = lax.Precision.HIGHEST


def slot_table(expert_ids, capacity):
    experts_axis = jnp.arange(EXPERTS, dtype=jnp.int32)
    counted = jnp.sum(
        (expert_ids[:, :, None] == experts_axis[None, None, :]).astype(jnp.int32), axis=1
    )
    ranking = jnp.cumsum(counted, axis=0) - 1
    places = jnp.arange(capacity, dtype=jnp.int32)
    slot_map = (counted.T[:, None, :] == 1) & (ranking.T[:, None, :] == places[None, :, None])
    return (counted, slot_map)


def slot_scales(slot_map, expert_ids, route_weight):
    experts_axis = jnp.arange(EXPERTS, dtype=jnp.int32)
    per_expert = jnp.sum(
        jnp.where(
            expert_ids[:, :, None] == experts_axis[None, None, :],
            route_weight[:, :, None],
            jnp.float32(0.0),
        ),
        axis=1,
    )
    return jnp.einsum("ect,te->ec", slot_map.astype(jnp.float32), per_expert, precision=exact_mode)


def place_rows(slot_map, scales, inputs, cotangents):
    selector = slot_map.astype(jnp.bfloat16)
    picked_inputs = jnp.einsum(
        "ect,td->ecd", selector, inputs, preferred_element_type=jnp.float32
    ).astype(jnp.bfloat16)
    picked_cot = jnp.einsum("ect,td->ecd", selector, cotangents, preferred_element_type=jnp.float32)
    scaled_cot = (scales[:, :, None] * picked_cot).astype(jnp.bfloat16)
    return (picked_inputs, scaled_cot)


def slot_grads(slot_inputs, slot_cotangents, paired, down_weight):
    hidden_width = down_weight.shape[0]
    joined = jnp.dot(slot_inputs, paired, preferred_element_type=jnp.float32)
    gate_pre = joined[:, :hidden_width]
    up_value = joined[:, hidden_width:]
    sigmoid_gate = jax.nn.sigmoid(gate_pre)
    active = gate_pre * sigmoid_gate
    hidden_grad = lax.dot_general(
        slot_cotangents, down_weight, (((1,), (1,)), ((), ())), preferred_element_type=jnp.float32
    )
    gate_grad = (
        hidden_grad * up_value * sigmoid_gate * (1.0 + gate_pre * (1.0 - sigmoid_gate))
    ).astype(jnp.bfloat16)
    up_grad = (hidden_grad * active).astype(jnp.bfloat16)
    stacked = jnp.concatenate([gate_grad, up_grad], axis=1)
    input_grad = lax.dot_general(
        stacked, paired, (((1,), (1,)), ((), ())), preferred_element_type=jnp.float32
    )
    return (input_grad, stacked)


def source_partials(slot_inputs, stacked, sources):
    capacity = slot_inputs.shape[0] // sources

    def accumulate(source, running):
        begin = (source * capacity).astype(jnp.int32)
        piece_inputs = lax.dynamic_slice_in_dim(slot_inputs, begin, capacity, 0)
        piece_grads = lax.dynamic_slice_in_dim(stacked, begin, capacity, 0)
        partial_sum = lax.dot_general(
            piece_inputs, piece_grads, (((0,), (0,)), ((), ())), preferred_element_type=jnp.float32
        )
        return running + lax.optimization_barrier(partial_sum.astype(jnp.bfloat16)).astype(
            jnp.float32
        )

    initial = jnp.zeros((slot_inputs.shape[1], stacked.shape[1]), jnp.float32)
    return lax.fori_loop(jnp.int32(0), jnp.int32(sources), accumulate, initial)


def body(tokens, cotangent, expert_ids, route_weight, w_gate, w_up, w_down):
    groups = lax.axis_size("group")
    hidden_width = w_gate.shape[2]
    counted, slot_map = slot_table(expert_ids, CAP)
    scales = slot_scales(slot_map, expert_ids, route_weight)
    paired_local = jnp.concatenate([w_gate, w_up], axis=2)
    sent_inputs, sent_cot = place_rows(slot_map, scales, tokens, cotangent)
    part_inputs, part_cot = (
        lax.all_to_all(sent_inputs, "group", split_axis=0, concat_axis=1, tiled=True),
        lax.all_to_all(sent_cot, "group", split_axis=0, concat_axis=1, tiled=True),
    )
    slot_inputs, slot_cot = (
        lax.all_gather(part_inputs, "shard", axis=2, tiled=True),
        lax.all_gather(part_cot, "shard", axis=2, tiled=True),
    )
    input_grad, stacked = slot_grads(slot_inputs[0], slot_cot[0], paired_local[0], w_down[0])
    grads_rows = [input_grad]
    weight_totals = [source_partials(slot_inputs[0], stacked, groups)]
    slot_grad = jnp.stack(grads_rows)
    summed_rows = lax.psum_scatter(slot_grad, "shard", scatter_dimension=2, tiled=True)
    returned = lax.all_to_all(summed_rows, "group", split_axis=1, concat_axis=0, tiled=True)
    grad_total = jnp.einsum(
        "ect,ecd->td", slot_map.astype(jnp.float32), returned, precision=exact_mode
    )
    stacked_totals = jnp.stack(weight_totals)
    grad_gate = stacked_totals[:, :, :hidden_width].astype(jnp.bfloat16)
    grad_up = stacked_totals[:, :, hidden_width:].astype(jnp.bfloat16)
    return (grad_total.astype(jnp.bfloat16), grad_gate, grad_up)


def solution(mesh):
    in_specs = (
        P("group", "shard"),
        P("group", "shard"),
        P("group", None),
        P("group", None),
        P("group", None, "shard"),
        P("group", None, "shard"),
        P("group", "shard", None),
    )
    out_specs = (P("group", "shard"), P("group", None, "shard"), P("group", None, "shard"))
    return jax.shard_map(body, mesh=mesh, in_specs=in_specs, out_specs=out_specs, check_vma=False)
```

profile of v0, /device:TPU:1, one launch (start us, length us, event | category | flops | bytes accessed | tf_op | source)
XLA Modules:
  0.0 811.4 jit_solution(8384122965178680824)
XLA Ops:
  7.2 0.0 copy-start
  7.2 0.0 all-gather.5.cloned.1.call-start
  7.2 0.8 convert_reduce_fusion
  8.0 0.1 copy.34
  8.1 0.1 reduce_window_sum.11
  8.2 0.1 copy.35
  8.2 0.9 convolution_convert_fusion.1
  9.1 0.1 reshape.42
  9.3 11.5 %all_to_all.36 = bf16[8,2,864]{2,1,0:T(2,128)(2,1)S(1)} all-to-all(bf16[8,2,864]{2,1,0:T(2,128)(2,1)S(1)} %reshape.42), channel_id=1, replica_groups=mesh['group'=8,'shard'=64] {'group'}, dimensions={0} | all-to-all | bytes 55296 | tf_op jit(solution)/shard_map/all_to_all | solution.py:92
  20.8 0.1 reshape.43
  21.0 0.7 copy.46
  21.7 0.0 all-gather.5.cloned.1.call-update
  21.7 0.0 all-gather.3.cloned.1.call-start
  21.7 0.7 select_reduce_fusion
  22.5 0.2 fusion.13
  22.7 0.9 fusion.5
  23.6 0.1 reshape.40
  23.7 7.5 all_to_all.37
  31.2 0.1 reshape.41
  31.3 0.7 copy.45
  32.1 0.0 all-gather.3.cloned.1.call-update
  32.1 0.0 all-reduce.3.cloned.1.call-start
  32.1 1.3 dynamic-slice
  34.1 76.7 %all-gather.5.cloned.1.call-done = bf16[1,288,3072]{1,2,0:T(8,128)(2,1)} async-done(((bf16[1,288,48]{1,2,0:T(8,128)(2,1)}), bf16[1,288,3072]{1,2,0:T(8,128)(2,1)}) %all-gather.5.cloned.1.call-update) | async-done | bytes 1769488 | tf_op jit(solution)/shard_map/all_gather | solution.py:96
  110.8 2.9 fusion.7
  113.7 82.8 %all-gather.3.cloned.1.call-done = bf16[1,288,3072]{1,2,0:T(8,128)(2,1)} async-done(((bf16[1,288,48]{1,2,0:T(8,128)(2,1)}), bf16[1,288,3072]{1,2,0:T(8,128)(2,1)}) %all-gather.3.cloned.1.call-update) | async-done | bytes 1769488 | tf_op jit(solution)/shard_map/all_gather | solution.py:97
  196.5 0.0 copy-done
  196.5 2.7 fusion.17
  199.2 2.4 convolution_bitcast_fusion
  201.6 2.4 copy.42
  204.0 10.6 %copy.38 = f32[1,288,3072]{1,0,2:T(1,128)} copy(f32[1,288,3072]{2,1,0:T(8,128)} %convolution_bitcast_fusion) | data formatting | bytes 7077888 | tf_op jit(solution)/shard_map/stack | solution.py:102
  214.6 0.0 all-reduce.3.cloned.1.call-update
  214.7 41.6 %while.11 = (s32[]{:T(128)}, f32[3072,256]{1,0:T(8,128)}, bf16[288,3072]{1,0:T(8,128)(2,1)}, bf16[288,256]{1,0:T(8,128)(2,1)S(1)}, s32[]{:T(128)}, /*index=5*/s32[]{:T(128)}, s32[]{:T(128)}, s32[]{:T(128)}) while((s32[]{:T(128)}, f32[3072,256]{1,0:T(8,128)}, bf16[288,3072]{1,0:T(8,128)(2,1)}, bf16[288,256]{1,0:T(8,128)(2,1)S(1)}, ...), condition=%wide.region_5.6_spmd.clone, body=%wide.region_4.5_spmd.clone.sunk | while | flops 59768836 | bytes 9704589 | solution.py:81
  214.7 1.6 convolution_convert_fusion.3
  216.3 1.9 select_add_fusion.2
  218.2 1.6 convolution_convert_fusion.3
  219.8 3.8 select_add_fusion.2
  223.7 1.6 convolution_convert_fusion.3
  225.3 3.8 select_add_fusion.2
  229.1 1.6 convolution_convert_fusion.3
  230.7 3.8 select_add_fusion.2
  234.5 1.6 convolution_convert_fusion.3
  236.1 3.9 select_add_fusion.2
  240.0 1.6 convolution_convert_fusion.3
  241.6 3.8 select_add_fusion.2
  245.4 1.6 convolution_convert_fusion.3
  247.0 3.8 select_add_fusion.2
  250.8 1.6 convolution_convert_fusion.3
  252.4 3.9 select_add_fusion.2
  256.3 2.0 convert_bitcast_fusion
  258.3 530.2 %all-reduce.3.cloned.1.call-done = f32[1,288,3072]{1,0,2:T(1,128)} async-done(((f32[1,288,3072]{1,0,2:T(1,128)}), f32[1,288,3072]{1,0,2:T(1,128)}) %all-reduce.3.cloned.1.call-update) | async-done | bytes 3538960
  788.6 0.9 constant_dynamic-slice_fusion
  789.5 0.1 copy.39
  789.6 0.5 broadcast.32
  790.1 1.0 reduce.5
  791.1 0.8 reshape.44
  791.9 4.2 all-to-all-start.2
  796.1 1.2 fusion.31
  797.3 4.0 all-to-all-done.2
  801.3 0.8 reduce.6
  802.1 0.3 reshape.45
  802.4 0.5 broadcast.31
  802.9 1.0 bitcast_reduce_fusion
  804.0 0.9 fusion.6
  (13 shorter events, 0.1 us)
Async XLA Ops:
  7.2 189.3 %copy-start = (bf16[1,128,3072]{2,1,0:T(8,128)(2,1)S(1)}, bf16[1,128,3072]{2,1,0:T(8,128)(2,1)}, u32[]{:S(2)}) copy-start(bf16[1,128,3072]{2,1,0:T(8,128)(2,1)} %param.15) | copy-start | bytes 2359300
  7.2 103.6 %all-gather.5.cloned.1.call-start = ((), (), s32[]{:S(2)}) async-start(), calls=%async_computation.4 | async-start | bytes 2396160 | tf_op jit(solution)/shard_map/all_gather | solution.py:96
  21.7 174.8 %all-gather.3.cloned.1.call-start = ((), (), s32[]{:S(2)}) async-start(), calls=%async_computation.3 | async-start | bytes 2396160 | tf_op jit(solution)/shard_map/all_gather | solution.py:97
  32.1 756.5 %all-reduce.3.cloned.1.call-start = ((), (), s32[]{:S(2)}) async-start(), calls=%async_computation.5 | async-start | bytes 9437184
  196.5 2.7 copy-start.2
  196.5 2.7 copy-start.3
  199.2 2.4 copy-start.1
  791.9 9.4 %all-to-all-start.2 = ((f32[8,1,1728]{2,1,0:T(1,128)}), f32[8,1,1728]{2,1,0:T(1,128)S(1)}, u32[]{:S(2)}, u32[]{:S(2)}) async-start(f32[8,1,1728]{2,1,0:T(1,128)} %reshape.44), calls=%async_computation.2 | async-start | bytes 114688 | tf_op jit(solution)/shard_map/all_to_all | solution.py:104
Sparse Core Ops, SparseCore 0:
  21.8 88.8 all-gather.4
  114.5 81.9 all-gather.2
  214.8 573.7 all-reduce.2
where the time goes:
time: 813 us; the launch traced here: 811 us
  waiting for transfers between devices  694 us (85%)
  other arithmetic  34.2 us (4%)
  matrix products  23.6 us (3%)
  local copies, waits for them, and re-layouts  21.8 us (3%)
  blocking collectives  19 us (2%)
  between operations  14.6 us (2%)
    unnamed x4, waiting for transfers between devices  530 us
    all_gather x1, waiting for transfers between devices, body(): lax.all_gather(part_cot, 'shard', axis=2, tiled=True)  82.8 us
    all_gather x1, waiting for transfers between devices, body(): lax.all_gather(part_inputs, 'shard', axis=2, tiled=True)  76.7 us
    add x8, other arithmetic, accumulate(): running + lax.optimization_barrier(partial_sum.astype(jnp.bfloat16)).asty...  28.8 us
  transfers between devices with their start and end apart: 4, of which 4 were waited for; matrix products, arithmetic and copies ran while one was open for 6% of the time, Pallas kernels for 0%

commit v1 on v0

--- a/solution.py
+++ b/solution.py
@@ -6,6 +6,11 @@
 EXPERTS = 8
 CAP = 36
 exact_mode = lax.Precision.HIGHEST
+
+
+def all_by_exchange(x, axis, dim):
+    sent = jnp.stack([x] * lax.axis_size(axis))
+    return jnp.concatenate(lax.all_to_all(sent, axis, 0, 0), axis=dim)
 
 
 def slot_table(expert_ids, capacity):
@@ -94,7 +99,7 @@
     )
     slot_inputs, slot_cot = (
         lax.all_gather(part_inputs, "shard", axis=2, tiled=True),
-        lax.all_gather(part_cot, "shard", axis=2, tiled=True),
+        all_by_exchange(part_cot, "shard", 2),
     )
     input_grad, stacked = slot_grads(slot_inputs[0], slot_cot[0], paired_local[0], w_down[0])
     grads_rows = [input_grad]

time: 813 us -> 773 us (0.951)
  waiting for transfers between devices: 694 us -> 638 us
  starting transfers between devices: 4.29 us -> 29.4 us
  blocking collectives: 19 us -> 7.46 us
    all_gather x1 -> x0, waiting for transfers between devices: 82.8 us -> none  [body(): lax.all_gather(part_cot, 'shard', axis=2, tiled=True)]
    all_to_all x0 -> x2, starting transfers between devices: none -> 25.1 us  [the longest x1 18.5 us: all_by_exchange(): return jnp.concatenate(lax.all_to_all(sent, axis, 0, 0), axis=dim)]
    all_gather x1, waiting for transfers between devices: 76.7 us -> 99.4 us  [body(): lax.all_gather(part_inputs, 'shard', axis=2, tiled=True)]
    all_to_all x1 -> x0, blocking collectives: 11.5 us -> none  [body(): lax.all_to_all(sent_inputs, 'group', split_axis=0, concat_axis=1, tiled=T...]
    unnamed x4 -> x3, waiting for transfers between devices: 530 us -> 530 us
  transfers between devices with their start and end apart: 4 -> 5, of which waited for: 4 -> 4; matrix products, arithmetic and copies ran while one was open for 6% -> 7% of each run, Pallas kernels for 0% -> 0%
where the time goes in v1:
time: 773 us; the launch traced here: 771 us
  waiting for transfers between devices  638 us (83%)
  other arithmetic  34.2 us (4%)
  starting transfers between devices  29.4 us (4%)
  matrix products  23.6 us (3%)
  local copies, waits for them, and re-layouts  23.4 us (3%)
  between operations  14.9 us (2%)
    unnamed x3, waiting for transfers between devices  530 us
    all_gather x1, waiting for transfers between devices, body(): lax.all_gather(part_inputs, 'shard', axis=2, tiled=True)  99.4 us
    add x8, other arithmetic, accumulate(): running + lax.optimization_barrier(partial_sum.astype(jnp.bfloat16)).asty...  28.8 us
    all_to_all x1, starting transfers between devices, all_by_exchange(): return jnp.concatenate(lax.all_to_all(sent, axis, 0, 0), axis=dim)  18.5 us
  transfers between devices with their start and end apart: 5, of which 4 were waited for; matrix products, arithmetic and copies ran while one was open for 7% of the time, Pallas kernels for 0%

profile of v1, /device:TPU:1, one launch (start us, length us, event | category | flops | bytes accessed | tf_op | source)
XLA Modules:
  0.0 771.0 jit_solution(11267570977507420075)
XLA Ops:
  7.2 0.0 copy-start
  7.2 0.8 convert_reduce_fusion
  7.9 0.1 copy.34
  8.0 0.1 reduce_window_sum.11
  8.1 0.1 copy.35
  8.2 0.9 convolution_convert_fusion.1
  9.1 0.7 reshape.51
  9.8 6.6 all-to-all-start.2
  16.5 0.0 all-gather.2.cloned.1.call-start
  16.5 0.7 select_reduce_fusion
  17.2 4.3 all-to-all-done.2
  21.6 0.1 reshape.52
  21.7 0.7 copy.46
  22.4 0.0 all-gather.2.cloned.1.call-update
  22.5 0.2 fusion.12
  22.7 0.9 fusion.3
  23.6 0.1 reshape.49
  23.7 7.5 all_to_all.38
  31.2 0.1 reshape.50
  31.4 0.1 copy.45
  31.5 1.6 stack.9
  33.1 18.5 %all-to-all-start.1 = ((bf16[64,1,288,48]{2,3,1,0:T(8,128)(2,1)}), bf16[64,1,288,48]{2,3,1,0:T(8,128)(2,1)S(1)}, u32[]{:S(2)}, u32[]{:S(2)}) async-start(bf16[64,1,288,48]{2,3,1,0:T(8,128)(2,1)} %stack.9), calls=%async_computation.1 | async-start | bytes 4718592 | tf_op jit(solution)/shard_map/all_to_all | solution.py:13
  51.5 0.0 all-reduce.3.cloned.1.call-start
  51.6 1.3 dynamic-slice
  53.5 99.4 %all-gather.2.cloned.1.call-done = bf16[1,288,3072]{1,2,0:T(8,128)(2,1)} async-done(((bf16[1,288,48]{1,2,0:T(8,128)(2,1)}), bf16[1,288,3072]{1,2,0:T(8,128)(2,1)}) %all-gather.2.cloned.1.call-update) | async-done | bytes 1769488 | tf_op jit(solution)/shard_map/all_gather | solution.py:101
  152.9 3.6 fusion.5
  156.5 0.0 copy-start.3
  156.5 2.0 fusion.16
  158.6 2.4 convolution_bitcast_fusion
  161.0 2.4 copy.42
  163.4 10.6 %copy.38 = f32[1,288,3072]{1,0,2:T(1,128)} copy(f32[1,288,3072]{2,1,0:T(8,128)} %convolution_bitcast_fusion) | data formatting | bytes 7077888 | tf_op jit(solution)/shard_map/stack | solution.py:107
  174.0 0.0 all-reduce.3.cloned.1.call-update
  174.0 41.6 %while.11 = (s32[]{:T(128)}, f32[3072,256]{1,0:T(8,128)}, bf16[288,3072]{1,0:T(8,128)(2,1)}, bf16[288,256]{1,0:T(8,128)(2,1)S(1)}, s32[]{:T(128)}, /*index=5*/s32[]{:T(128)}, s32[]{:T(128)}, s32[]{:T(128)}) while((s32[]{:T(128)}, f32[3072,256]{1,0:T(8,128)}, bf16[288,3072]{1,0:T(8,128)(2,1)}, bf16[288,256]{1,0:T(8,128)(2,1)S(1)}, ...), condition=%wide.region_5.6_spmd.clone, body=%wide.region_4.5_spmd.clone.sunk | while | flops 59768836 | bytes 9704589 | solution.py:86
  174.1 1.6 convolution_convert_fusion.3
  175.7 1.9 select_add_fusion.2
  177.6 1.6 convolution_convert_fusion.3
  179.2 3.8 select_add_fusion.2
  183.0 1.6 convolution_convert_fusion.3
  184.6 3.8 select_add_fusion.2
  188.5 1.6 convolution_convert_fusion.3
  190.1 3.8 select_add_fusion.2
  193.9 1.6 convolution_convert_fusion.3
  195.5 3.9 select_add_fusion.2
  199.4 1.6 convolution_convert_fusion.3
  201.0 3.8 select_add_fusion.2
  204.8 1.6 convolution_convert_fusion.3
  206.4 3.8 select_add_fusion.2
  210.2 1.6 convolution_convert_fusion.3
  211.8 3.9 select_add_fusion.2
  215.7 2.0 convert_bitcast_fusion
  217.7 530.2 %all-reduce.3.cloned.1.call-done = f32[1,288,3072]{1,0,2:T(1,128)} async-done(((f32[1,288,3072]{1,0,2:T(1,128)}), f32[1,288,3072]{1,0,2:T(1,128)}) %all-reduce.3.cloned.1.call-update) | async-done | bytes 3538960
  747.9 0.9 constant_dynamic-slice_fusion
  748.8 0.1 copy.39
  748.9 0.5 broadcast.34
  749.4 1.0 reduce.5
  750.4 0.8 reshape.53
  751.2 4.2 all-to-all-start.3
  755.4 1.2 fusion.30
  756.6 4.0 all-to-all-done.3
  760.7 0.8 reduce.6
  761.4 0.3 reshape.54
  761.7 0.5 broadcast.33
  762.2 1.0 bitcast_reduce_fusion
  763.3 0.9 fusion.4
  (14 shorter events, 0.1 us)
Async XLA Ops:
  7.2 149.4 %copy-start = (bf16[1,128,3072]{2,1,0:T(8,128)(2,1)S(1)}, bf16[1,128,3072]{2,1,0:T(8,128)(2,1)}, u32[]{:S(2)}) copy-start(bf16[1,128,3072]{2,1,0:T(8,128)(2,1)} %param.15) | copy-start | bytes 2359300
  9.8 11.7 %all-to-all-start.2 = ((bf16[8,2,864]{2,1,0:T(2,128)(2,1)}), bf16[8,2,864]{2,1,0:T(2,128)(2,1)S(1)}, u32[]{:S(2)}, u32[]{:S(2)}) async-start(bf16[8,2,864]{2,1,0:T(2,128)(2,1)} %reshape.51), calls=%async_computation.2 | async-start | bytes 57344 | tf_op jit(solution)/shard_map/all_to_all | solution.py:97
  16.5 136.4 %all-gather.2.cloned.1.call-start = ((), (), s32[]{:S(2)}) async-start(), calls=%async_computation.4 | async-start | bytes 2396160 | tf_op jit(solution)/shard_map/all_gather | solution.py:101
  33.1 123.5 %all-to-all-start.1 = ((bf16[64,1,288,48]{2,3,1,0:T(8,128)(2,1)}), bf16[64,1,288,48]{2,3,1,0:T(8,128)(2,1)S(1)}, u32[]{:S(2)}, u32[]{:S(2)}) async-start(bf16[64,1,288,48]{2,3,1,0:T(8,128)(2,1)} %stack.9), calls=%async_computation.1 | async-start | bytes 4718592 | tf_op jit(solution)/shard_map/all_to_all | solution.py:13
  51.5 696.3 %all-reduce.3.cloned.1.call-start = ((), (), s32[]{:S(2)}) async-start(), calls=%async_computation.5 | async-start | bytes 9437184
  156.5 2.0 copy-start.2
  156.5 2.0 copy-start.3
  158.6 2.4 copy-start.1
  751.2 9.4 %all-to-all-start.3 = ((f32[8,1,1728]{2,1,0:T(1,128)}), f32[8,1,1728]{2,1,0:T(1,128)S(1)}, u32[]{:S(2)}, u32[]{:S(2)}) async-start(f32[8,1,1728]{2,1,0:T(1,128)} %reshape.53), calls=%async_computation.3 | async-start | bytes 114688 | tf_op jit(solution)/shard_map/all_to_all | solution.py:109
Sparse Core Ops, SparseCore 0:
  22.6 130.2 all-gather.1
  174.2 573.6 all-reduce.2
